TPU v7x, 256 devices: a whole 4x4x8 slice. The times are simulated.
256 devices in a mesh: section: 2 (over core), ctx: 128 (over y, z, x).
Axes of the slice: x: 4, y: 4, z: 8, core: 2. Of those that a mesh axis runs over, the one named last changes fastest.
Arguments:
- queries: bfloat16 [2, 8192, 4096], P('section', 'ctx'), may hold values from -80 to 80
- key_rows: bfloat16 [2, 8192, 512], P('section', 'ctx'), may hold values from -8 to 8
- rows_of_value: bfloat16 [2, 8192, 512], P('section', 'ctx'), may hold values from -6 to 6
- query_gain: float32 [4096], replicated, may hold values from 2 to 6
- block_order: int32 [256], replicated, may hold values from 0 to 255, each once
Outputs:
- attended: bfloat16 [2, 8192, 4096], P('section', 'ctx')
Inputs may be any that keep to these rules, and one draw needn't show every extreme that they name: A permutation; stored block j of 32 rows holds the sequence's block block_order[j].
All inputs are finite; a program needn't handle non-finite values.
Results may differ from a plain program's by a relative error of at most 0.0085.
Values may be sent and summed in bfloat16 or wider, within the bound.
A program may use at most 192 MiB of HBM per device.

v0:
```python
import math
import jax
import jax.numpy as jnp
from jax import lax
from jax.sharding import PartitionSpec as P

HEAD_SIZE = 128
QUERY_PER_GROUP = 8


def from_behind(value, axis, steps):
    count = lax.axis_size(axis)
    initial, last = (max(0, -steps), min(count, count - steps))
    return lax.ppermute(value, axis, [(source, source + steps) for source in range(initial, last)])


def key_positions(block_order, first_row_index, row_count, block_rows):
    row_ids = first_row_index + jnp.arange(row_count, dtype=jnp.int32)
    slot_ids = row_ids // block_rows
    slot_table = jnp.arange(block_order.shape[0], dtype=jnp.int32)
    picked = jnp.sum(
        jnp.where(slot_ids[:, None] == slot_table[None, :], block_order[None, :], 0), axis=1
    )
    return picked * block_rows + row_ids % block_rows


def fold_step(carry_state, key_piece, value_piece, key_pos, query_four, query_pos, needed):
    row_count = key_piece.shape[0]
    kv_heads = query_four.shape[1]
    score_scale = 1.0 / math.sqrt(HEAD_SIZE)

    def compute(old_state):
        row_max, row_sum, mixed_sum = old_state
        key_quad = key_piece.reshape(row_count, kv_heads, HEAD_SIZE)
        scores = (
            jnp.einsum("qjgd,kjd->jgqk", query_four, key_quad, preferred_element_type=jnp.float32)
            * score_scale
        )
        scores = jnp.where(key_pos[None, :] <= query_pos[:, None], scores, -jnp.inf)
        new_max = jnp.maximum(row_max, jnp.max(scores, axis=-1))
        rescale = jnp.exp(row_max - new_max)
        weights = jnp.exp(scores - new_max[..., None])
        new_sum = row_sum * rescale + jnp.sum(weights, axis=-1)
        value_four = value_piece.reshape(row_count, kv_heads, HEAD_SIZE)
        product = jnp.einsum(
            "jgqk,kjd->qjgd",
            weights.astype(jnp.bfloat16),
            value_four,
            preferred_element_type=jnp.float32,
        )
        new_mixed = mixed_sum * jnp.transpose(rescale, (2, 0, 1))[..., None] + product
        return (new_max, new_sum, new_mixed)

    return lax.cond(needed, compute, lambda same_state: same_state, carry_state)


def body(queries, key_rows, rows_of_value, query_gain, block_order):
    rows_here = queries.shape[1]
    block_rows = rows_here // 2
    query_pos = key_positions(block_order, lax.axis_index("ctx") * rows_here, rows_here, block_rows)
    section_now = lax.axis_index("section")
    kv_heads = key_rows.shape[2] // HEAD_SIZE
    column_count = queries.shape[2]
    start_state = (
        jnp.full((kv_heads, QUERY_PER_GROUP, rows_here), -1e30, jnp.float32),
        jnp.zeros((kv_heads, QUERY_PER_GROUP, rows_here), jnp.float32),
        jnp.zeros((rows_here, kv_heads, QUERY_PER_GROUP, HEAD_SIZE), jnp.float32),
    )

    def finish(final_state):
        row_max, row_sum, mixed_sum = final_state
        safe_sum = jnp.where(row_sum > 0.0, row_sum, 1.0)
        mixed_out = mixed_sum / jnp.transpose(safe_sum, (2, 0, 1))[..., None]
        return mixed_out.reshape(rows_here, column_count).astype(jnp.bfloat16)

    gathered = (
        lax.all_gather(key_rows, "ctx", axis=1, tiled=True),
        lax.all_gather(rows_of_value, "ctx", axis=1, tiled=True),
    )
    total_rows = gathered[0].shape[1]
    width_of_block = math.gcd(total_rows, 512)

    def attend(rows_of_query, active):
        query_four = rows_of_query.reshape(rows_here, kv_heads, QUERY_PER_GROUP, HEAD_SIZE)

        def loop_body(loop_index, carry_state):
            first_row_index = loop_index * width_of_block
            key_piece = lax.dynamic_slice_in_dim(gathered[0][0], first_row_index, width_of_block, 0)
            value_piece = lax.dynamic_slice_in_dim(
                gathered[1][0], first_row_index, width_of_block, 0
            )
            key_pos = key_positions(block_order, first_row_index, width_of_block, block_rows)
            return fold_step(
                carry_state, key_piece, value_piece, key_pos, query_four, query_pos, active
            )

        return finish(lax.fori_loop(0, total_rows // width_of_block, loop_body, start_state))

    first_out = attend(queries[0], section_now == 0)
    received = from_behind(first_out, "section", 1)
    shifted = (
        queries[0].astype(jnp.float32) + query_gain[None, :] * received.astype(jnp.float32)
    ).astype(jnp.bfloat16)
    second = attend(shifted, section_now == 1)
    result = jnp.where(section_now == 0, first_out, second)
    return result[None]


def solution(mesh):
    placed = (
        P("section", "ctx", None),
        P("section", "ctx", None),
        P("section", "ctx", None),
        P(),
        P(),
    )
    return jax.shard_map(
        body, mesh=mesh, in_specs=placed, out_specs=P("section", "ctx", None), check_vma=False
    )
```

profile of v0, /device:TPU:1, one launch (start us, length us, event | category | flops | bytes accessed | tf_op | source)
XLA Modules:
  0.0 462.5 jit_solution(13137162699228120019)
XLA Ops:
  10.3 125.7 %all-gather.3.cloned.1.call-done = bf16[1,8192,512]{2,1,0:T(8,128)(2,1)} async-done(((bf16[1,64,512]{2,1,0:T(8,128)(2,1)}), bf16[1,8192,512]{2,1,0:T(8,128)(2,1)}) %all-gather.3.cloned.1.call-update) | async-done | bytes 8388624 | tf_op jit(solution)/shard_map/all_gather | solution.py:77
  135.9 12.0 %copy.33 = bf16[1,8192,512]{1,2,0:T(8,128)(2,1)} copy(bf16[1,8192,512]{2,1,0:T(8,128)(2,1)} %all-gather.3.cloned.1.call-done) | data formatting | bytes 16777216 | tf_op jit(solution)/shard_map/while | solution.py:97
  147.9 112.4 %all-gather.5.cloned.1.call-done = bf16[1,8192,512]{2,1,0:T(8,128)(2,1)} async-done(((bf16[1,64,512]{2,1,0:T(8,128)(2,1)}), bf16[1,8192,512]{2,1,0:T(8,128)(2,1)}) %all-gather.5.cloned.1.call-update) | async-done | bytes 8388624 | tf_op jit(solution)/shard_map/all_gather | solution.py:78
  260.3 11.9 %copy.35 = bf16[1,8192,512]{1,2,0:T(8,128)(2,1)} copy(bf16[1,8192,512]{2,1,0:T(8,128)(2,1)} %all-gather.5.cloned.1.call-done) | data formatting | bytes 16777216 | tf_op jit(solution)/shard_map/while | solution.py:97
  272.4 1.7 while.38
  275.1 1.5 collective-permute-start
  276.6 89.6 %collective-permute-done = bf16[64,4096]{1,0:T(8,128)(2,1)S(1)} collective-permute-done((bf16[64,4096]{1,0:T(8,128)(2,1)S(1)}, bf16[64,4096]{1,0:T(8,128)(2,1)S(1)}, u32[]{:S(2)}, u32[]{:S(2)}) %collective-permute-start) | collective-permute-done | bytes 524320 | tf_op jit(solution)/shard_map/ppermute | solution.py:14
  366.7 86.8 %while.39 = (s32[]{:T(128)}, f32[4,8,64]{2,1,0:T(8,128)S(1)}, f32[4,8,64]{2,1,0:T(8,128)S(1)}, f32[64,4,8,128]{3,0,2,1:T(8,128)S(1)}, pred[]{:T(512)}, /*index=5...) while((s32[]{:T(128)}, f32[4,8,64]{2,1,0:T(8,128)S(1)}, ...), condition=%wide.region_14.15_spmd, body=%wide.region_8.14_spmd.sunk | while | flops 549376512 | bytes 19682900 | solution.py:97
  366.8 5.3 %conditional.5 = ((f32[4,8,64]{2,1,0:T(8,128)S(1)}, f32[4,8,64]{2,1,0:T(8,128)S(1)}, f32[64,4,8,128]{3,0,2,1:T(8,128)S(1)})) conditional(s32[]{:T(128)} %convert_element_type.110, (f32[4,8,64]{2,1,0:T(8,128)S(1)}, f32[4,8,64]{2,1,0:T(8,128)S(1)}, f32[64,4,8,128]{3,0,2,1:T(8,128)S(1)}) %tuple.209, (s32[]{:T(128)}, ...), branch_computations={%region_9.9_spmd, %region_10.13_spmd.clone.clone} | conditional | flops 549376512 | bytes 19154254 | solution.py:54
  369.3 1.5 fusion.32
  370.8 1.3 fusion.21
  372.3 5.3 %conditional.5 = ((f32[4,8,64]{2,1,0:T(8,128)S(1)}, f32[4,8,64]{2,1,0:T(8,128)S(1)}, f32[64,4,8,128]{3,0,2,1:T(8,128)S(1)})) conditional(s32[]{:T(128)} %convert_element_type.110, (f32[4,8,64]{2,1,0:T(8,128)S(1)}, f32[4,8,64]{2,1,0:T(8,128)S(1)}, f32[64,4,8,128]{3,0,2,1:T(8,128)S(1)}) %tuple.209, (s32[]{:T(128)}, ...), branch_computations={%region_9.9_spmd, %region_10.13_spmd.clone.clone} | conditional | flops 549376512 | bytes 19154254 | solution.py:54
  374.7 1.5 fusion.32
  376.3 1.3 fusion.21
  377.7 5.3 %conditional.5 = ((f32[4,8,64]{2,1,0:T(8,128)S(1)}, f32[4,8,64]{2,1,0:T(8,128)S(1)}, f32[64,4,8,128]{3,0,2,1:T(8,128)S(1)})) conditional(s32[]{:T(128)} %convert_element_type.110, (f32[4,8,64]{2,1,0:T(8,128)S(1)}, f32[4,8,64]{2,1,0:T(8,128)S(1)}, f32[64,4,8,128]{3,0,2,1:T(8,128)S(1)}) %tuple.209, (s32[]{:T(128)}, ...), branch_computations={%region_9.9_spmd, %region_10.13_spmd.clone.clone} | conditional | flops 549376512 | bytes 19154254 | solution.py:54
  380.2 1.5 fusion.32
  381.7 1.3 fusion.21
  383.1 5.3 %conditional.5 = ((f32[4,8,64]{2,1,0:T(8,128)S(1)}, f32[4,8,64]{2,1,0:T(8,128)S(1)}, f32[64,4,8,128]{3,0,2,1:T(8,128)S(1)})) conditional(s32[]{:T(128)} %convert_element_type.110, (f32[4,8,64]{2,1,0:T(8,128)S(1)}, f32[4,8,64]{2,1,0:T(8,128)S(1)}, f32[64,4,8,128]{3,0,2,1:T(8,128)S(1)}) %tuple.209, (s32[]{:T(128)}, ...), branch_computations={%region_9.9_spmd, %region_10.13_spmd.clone.clone} | conditional | flops 549376512 | bytes 19154254 | solution.py:54
  385.6 1.5 fusion.32
  387.1 1.3 fusion.21
  388.5 5.3 %conditional.5 = ((f32[4,8,64]{2,1,0:T(8,128)S(1)}, f32[4,8,64]{2,1,0:T(8,128)S(1)}, f32[64,4,8,128]{3,0,2,1:T(8,128)S(1)})) conditional(s32[]{:T(128)} %convert_element_type.110, (f32[4,8,64]{2,1,0:T(8,128)S(1)}, f32[4,8,64]{2,1,0:T(8,128)S(1)}, f32[64,4,8,128]{3,0,2,1:T(8,128)S(1)}) %tuple.209, (s32[]{:T(128)}, ...), branch_computations={%region_9.9_spmd, %region_10.13_spmd.clone.clone} | conditional | flops 549376512 | bytes 19154254 | solution.py:54
  391.0 1.5 fusion.32
  392.5 1.3 fusion.21
  394.0 5.3 %conditional.5 = ((f32[4,8,64]{2,1,0:T(8,128)S(1)}, f32[4,8,64]{2,1,0:T(8,128)S(1)}, f32[64,4,8,128]{3,0,2,1:T(8,128)S(1)})) conditional(s32[]{:T(128)} %convert_element_type.110, (f32[4,8,64]{2,1,0:T(8,128)S(1)}, f32[4,8,64]{2,1,0:T(8,128)S(1)}, f32[64,4,8,128]{3,0,2,1:T(8,128)S(1)}) %tuple.209, (s32[]{:T(128)}, ...), branch_computations={%region_9.9_spmd, %region_10.13_spmd.clone.clone} | conditional | flops 549376512 | bytes 19154254 | solution.py:54
  396.4 1.5 fusion.32
  397.9 1.3 fusion.21
  399.4 5.3 %conditional.5 = ((f32[4,8,64]{2,1,0:T(8,128)S(1)}, f32[4,8,64]{2,1,0:T(8,128)S(1)}, f32[64,4,8,128]{3,0,2,1:T(8,128)S(1)})) conditional(s32[]{:T(128)} %convert_element_type.110, (f32[4,8,64]{2,1,0:T(8,128)S(1)}, f32[4,8,64]{2,1,0:T(8,128)S(1)}, f32[64,4,8,128]{3,0,2,1:T(8,128)S(1)}) %tuple.209, (s32[]{:T(128)}, ...), branch_computations={%region_9.9_spmd, %region_10.13_spmd.clone.clone} | conditional | flops 549376512 | bytes 19154254 | solution.py:54
  401.8 1.5 fusion.32
  404.8 5.3 %conditional.5 = ((f32[4,8,64]{2,1,0:T(8,128)S(1)}, f32[4,8,64]{2,1,0:T(8,128)S(1)}, f32[64,4,8,128]{3,0,2,1:T(8,128)S(1)})) conditional(s32[]{:T(128)} %convert_element_type.110, (f32[4,8,64]{2,1,0:T(8,128)S(1)}, f32[4,8,64]{2,1,0:T(8,128)S(1)}, f32[64,4,8,128]{3,0,2,1:T(8,128)S(1)}) %tuple.209, (s32[]{:T(128)}, ...), branch_computations={%region_9.9_spmd, %region_10.13_spmd.clone.clone} | conditional | flops 549376512 | bytes 19154254 | solution.py:54
  407.3 1.5 fusion.32
  410.2 5.3 %conditional.5 = ((f32[4,8,64]{2,1,0:T(8,128)S(1)}, f32[4,8,64]{2,1,0:T(8,128)S(1)}, f32[64,4,8,128]{3,0,2,1:T(8,128)S(1)})) conditional(s32[]{:T(128)} %convert_element_type.110, (f32[4,8,64]{2,1,0:T(8,128)S(1)}, f32[4,8,64]{2,1,0:T(8,128)S(1)}, f32[64,4,8,128]{3,0,2,1:T(8,128)S(1)}) %tuple.209, (s32[]{:T(128)}, ...), branch_computations={%region_9.9_spmd, %region_10.13_spmd.clone.clone} | conditional | flops 549376512 | bytes 19154254 | solution.py:54
  412.7 1.5 fusion.32
  415.6 5.3 %conditional.5 = ((f32[4,8,64]{2,1,0:T(8,128)S(1)}, f32[4,8,64]{2,1,0:T(8,128)S(1)}, f32[64,4,8,128]{3,0,2,1:T(8,128)S(1)})) conditional(s32[]{:T(128)} %convert_element_type.110, (f32[4,8,64]{2,1,0:T(8,128)S(1)}, f32[4,8,64]{2,1,0:T(8,128)S(1)}, f32[64,4,8,128]{3,0,2,1:T(8,128)S(1)}) %tuple.209, (s32[]{:T(128)}, ...), branch_computations={%region_9.9_spmd, %region_10.13_spmd.clone.clone} | conditional | flops 549376512 | bytes 19154254 | solution.py:54
  418.1 1.5 fusion.32
  421.1 5.3 %conditional.5 = ((f32[4,8,64]{2,1,0:T(8,128)S(1)}, f32[4,8,64]{2,1,0:T(8,128)S(1)}, f32[64,4,8,128]{3,0,2,1:T(8,128)S(1)})) conditional(s32[]{:T(128)} %convert_element_type.110, (f32[4,8,64]{2,1,0:T(8,128)S(1)}, f32[4,8,64]{2,1,0:T(8,128)S(1)}, f32[64,4,8,128]{3,0,2,1:T(8,128)S(1)}) %tuple.209, (s32[]{:T(128)}, ...), branch_computations={%region_9.9_spmd, %region_10.13_spmd.clone.clone} | conditional | flops 549376512 | bytes 19154254 | solution.py:54
  423.5 1.5 fusion.32
  426.5 5.3 %conditional.5 = ((f32[4,8,64]{2,1,0:T(8,128)S(1)}, f32[4,8,64]{2,1,0:T(8,128)S(1)}, f32[64,4,8,128]{3,0,2,1:T(8,128)S(1)})) conditional(s32[]{:T(128)} %convert_element_type.110, (f32[4,8,64]{2,1,0:T(8,128)S(1)}, f32[4,8,64]{2,1,0:T(8,128)S(1)}, f32[64,4,8,128]{3,0,2,1:T(8,128)S(1)}) %tuple.209, (s32[]{:T(128)}, ...), branch_computations={%region_9.9_spmd, %region_10.13_spmd.clone.clone} | conditional | flops 549376512 | bytes 19154254 | solution.py:54
  429.0 1.5 fusion.32
  431.9 5.3 %conditional.5 = ((f32[4,8,64]{2,1,0:T(8,128)S(1)}, f32[4,8,64]{2,1,0:T(8,128)S(1)}, f32[64,4,8,128]{3,0,2,1:T(8,128)S(1)})) conditional(s32[]{:T(128)} %convert_element_type.110, (f32[4,8,64]{2,1,0:T(8,128)S(1)}, f32[4,8,64]{2,1,0:T(8,128)S(1)}, f32[64,4,8,128]{3,0,2,1:T(8,128)S(1)}) %tuple.209, (s32[]{:T(128)}, ...), branch_computations={%region_9.9_spmd, %region_10.13_spmd.clone.clone} | conditional | flops 549376512 | bytes 19154254 | solution.py:54
  434.4 1.5 fusion.32
  435.9 1.3 fusion.21
  437.3 5.3 %conditional.5 = ((f32[4,8,64]{2,1,0:T(8,128)S(1)}, f32[4,8,64]{2,1,0:T(8,128)S(1)}, f32[64,4,8,128]{3,0,2,1:T(8,128)S(1)})) conditional(s32[]{:T(128)} %convert_element_type.110, (f32[4,8,64]{2,1,0:T(8,128)S(1)}, f32[4,8,64]{2,1,0:T(8,128)S(1)}, f32[64,4,8,128]{3,0,2,1:T(8,128)S(1)}) %tuple.209, (s32[]{:T(128)}, ...), branch_computations={%region_9.9_spmd, %region_10.13_spmd.clone.clone} | conditional | flops 549376512 | bytes 19154254 | solution.py:54
  439.8 1.5 fusion.32
  441.3 1.3 fusion.21
  442.8 5.3 %conditional.5 = ((f32[4,8,64]{2,1,0:T(8,128)S(1)}, f32[4,8,64]{2,1,0:T(8,128)S(1)}, f32[64,4,8,128]{3,0,2,1:T(8,128)S(1)})) conditional(s32[]{:T(128)} %convert_element_type.110, (f32[4,8,64]{2,1,0:T(8,128)S(1)}, f32[4,8,64]{2,1,0:T(8,128)S(1)}, f32[64,4,8,128]{3,0,2,1:T(8,128)S(1)}) %tuple.209, (s32[]{:T(128)}, ...), branch_computations={%region_9.9_spmd, %region_10.13_spmd.clone.clone} | conditional | flops 549376512 | bytes 19154254 | solution.py:54
  445.2 1.5 fusion.32
  448.2 5.3 %conditional.5 = ((f32[4,8,64]{2,1,0:T(8,128)S(1)}, f32[4,8,64]{2,1,0:T(8,128)S(1)}, f32[64,4,8,128]{3,0,2,1:T(8,128)S(1)})) conditional(s32[]{:T(128)} %convert_element_type.110, (f32[4,8,64]{2,1,0:T(8,128)S(1)}, f32[4,8,64]{2,1,0:T(8,128)S(1)}, f32[64,4,8,128]{3,0,2,1:T(8,128)S(1)}) %tuple.209, (s32[]{:T(128)}, ...), branch_computations={%region_9.9_spmd, %region_10.13_spmd.clone.clone} | conditional | flops 549376512 | bytes 19154254 | solution.py:54
  450.7 1.5 fusion.32
  (296 shorter events, 58.4 us)
Async XLA Ops:
  6.5 129.4 %all-gather.3.cloned.1.call-start = ((), (), s32[]{:S(2)}) async-start(), calls=%async_computation | async-start | bytes 8454144 | tf_op jit(solution)/shard_map/all_gather | solution.py:77
  7.3 253.0 %all-gather.5.cloned.1.call-start = ((), (), s32[]{:S(2)}) async-start(), calls=%async_computation.1 | async-start | bytes 8454144 | tf_op jit(solution)/shard_map/all_gather | solution.py:78
  147.9 124.5 %copy-start.1 = (s32[256]{0:T(256)S(1)}, s32[256]{0:T(256)}, u32[]{:S(2)}) copy-start(s32[256]{0:T(256)} %param.17) | copy-start | bytes 3076
  272.4 93.7 %copy-start = (bf16[1,64,4096]{2,1,0:T(8,128)(2,1)S(1)}, bf16[1,64,4096]{2,1,0:T(8,128)(2,1)}, u32[]{:S(2)}) copy-start(bf16[1,64,4096]{2,1,0:T(8,128)(2,1)} %param.13) | copy-start | bytes 1572868
  272.4 93.7 %copy-start.2 = (f32[4096]{0:T(1024)S(1)}, f32[4096]{0:T(1024)}, u32[]{:S(2)}) copy-start(f32[4096]{0:T(1024)} %param.16) | copy-start | bytes 49156
  275.1 91.0 %collective-permute-start = (bf16[64,4096]{1,0:T(8,128)(2,1)S(1)}, bf16[64,4096]{1,0:T(8,128)(2,1)S(1)}, u32[]{:S(2)}, u32[]{:S(2)}) collective-permute-start(bf16[64,4096]{1,0:T(8,128)(2,1)S(1)} %bitcast.108), channel_id=1, source_target_pairs={{0,128},{1,129},{2,130},{3,131},{4,132},{5,133},{6,134},{7,135},{8... | collective-permute-start | bytes 1572872 | tf_op jit(solution)/shard_map/ppermute | solution.py:14
Sparse Core Ops, SparseCore 0:
  11.0 124.9 all-gather.2
  139.5 120.6 all-gather.4
where the time goes:
time: 464 us; the launch traced here: 462 us
  waiting for transfers between devices  329 us (71%)
  local copies, waits for them, and re-layouts  49.6 us (11%)
  matrix products  36.7 us (8%)
  other arithmetic  29 us (6%)
  between operations  13.6 us (3%)
    all_gather x1, waiting for transfers between devices, body(): lax.all_gather(key_rows, 'ctx', axis=1, tiled=True)  126 us
    all_gather x1, waiting for transfers between devices, body(): lax.all_gather(rows_of_value, 'ctx', axis=1, tiled=True)  112 us
    ppermute x1, waiting for transfers between devices, from_behind(): lax.ppermute(value, axis, [(source, source + steps) for source in range(i...  89.6 us
    while x4, local copies, waits for them, and re-layouts, attend(): lax.fori_loop(0, total_rows // width_of_block, loop_body, start_state)  24.3 us
    dot_general x16, matrix products, compute(): jnp.einsum('jgqk,kjd->qjgd', weights.astype(jnp.bfloat16), value_four, pr...  24.2 us
    reduce_sum x16, other arithmetic, compute(): new_sum = row_sum * rescale + jnp.sum(weights, axis=-1)  20.8 us
    dynamic_slice x16, local copies, waits for them, and re-layouts, loop_body(): lax.dynamic_slice_in_dim(gathered[0][0], first_row_index, width_of_block, 0)  20.4 us
    dot_general x16, matrix products, compute(): jnp.einsum('qjgd,kjd->jgqk', query_four, key_quad, preferred_element_type...  12.4 us
  transfers between devices with their start and end apart: 3, of which 3 were waited for; matrix products, arithmetic and copies ran while one was open for 3% of the time, Pallas kernels for 0%

commit v1 on v0

--- a/solution.py
+++ b/solution.py
@@ -75,7 +75,9 @@
 
     gathered = (
         lax.all_gather(key_rows, "ctx", axis=1, tiled=True),
-        lax.all_gather(rows_of_value, "ctx", axis=1, tiled=True),
+        jnp.concatenate(
+            lax.all_to_all(jnp.stack([rows_of_value] * lax.axis_size("ctx")), "ctx", 0, 0), axis=1
+        ),
     )
     total_rows = gathered[0].shape[1]
     width_of_block = math.gcd(total_rows, 512)

time: 464 us -> 622 us (1.34)
  matrix products: 36.7 us -> 119 us
  waiting for transfers between devices: 329 us -> 376 us
  starting transfers between devices: 1.51 us -> 18.5 us
  local copies, waits for them, and re-layouts: 49.6 us -> 60.4 us
    all_gather x1 -> x0, waiting for transfers between devices: 112 us -> none  [body(): lax.all_gather(rows_of_value, 'ctx', axis=1, tiled=True)]
    ppermute x1, waiting for transfers between devices: 89.6 us -> 171 us  [from_behind(): lax.ppermute(value, axis, [(source, source + steps) for source in range(i...]
    all_gather x1, waiting for transfers between devices: 126 us -> 201 us  [body(): lax.all_gather(key_rows, 'ctx', axis=1, tiled=True)]
    dot_general x16, matrix products: 24.2 us -> 77.3 us  [compute(): jnp.einsum('jgqk,kjd->qjgd', weights.astype(jnp.bfloat16), value_four, pr...]
    dot_general x16, matrix products: 12.4 us -> 42.1 us  [compute(): jnp.einsum('qjgd,kjd->jgqk', query_four, key_quad, preferred_element_type...]
    dynamic_slice x0 -> x32, local copies, waits for them, and re-layouts: none -> 20.7 us  [loop_body(): lax.dynamic_slice_in_dim(gathered[1][0], first_row_index, width_of_block, 0)]
    all_to_all x0 -> x1, starting transfers between devices: none -> 17 us  [body(): lax.all_to_all(jnp.stack([rows_of_value] * lax.axis_size('ctx')), 'ctx',...]
    while x4 -> x3, local copies, waits for them, and re-layouts: 24.3 us -> 12.3 us  [attend(): lax.fori_loop(0, total_rows // width_of_block, loop_body, start_state)]
where the time goes in v1:
time: 622 us; the launch traced here: 620 us
  waiting for transfers between devices  376 us (60%)
  matrix products  119 us (19%)
  local copies, waits for them, and re-layouts  60.4 us (10%)
  other arithmetic  29.3 us (5%)
  starting transfers between devices  18.5 us (3%)
  between operations  13.6 us (2%)
    all_gather x1, waiting for transfers between devices, body(): lax.all_gather(key_rows, 'ctx', axis=1, tiled=True)  201 us
    ppermute x1, waiting for transfers between devices, from_behind(): lax.ppermute(value, axis, [(source, source + steps) for source in range(i...  171 us
    dot_general x16, matrix products, compute(): jnp.einsum('jgqk,kjd->qjgd', weights.astype(jnp.bfloat16), value_four, pr...  77.3 us
    dot_general x16, matrix products, compute(): jnp.einsum('qjgd,kjd->jgqk', query_four, key_quad, preferred_element_type...  42.1 us
    reduce_sum x16, other arithmetic, compute(): new_sum = row_sum * rescale + jnp.sum(weights, axis=-1)  20.8 us
    dynamic_slice x32, local copies, waits for them, and re-layouts, loop_body(): lax.dynamic_slice_in_dim(gathered[1][0], first_row_index, width_of_block, 0)  20.7 us
    dynamic_slice x16, local copies, waits for them, and re-layouts, loop_body(): lax.dynamic_slice_in_dim(gathered[0][0], first_row_index, width_of_block, 0)  17.3 us
    all_to_all x1, starting transfers between devices, body(): lax.all_to_all(jnp.stack([rows_of_value] * lax.axis_size('ctx')), 'ctx',...  17 us
  transfers between devices with their start and end apart: 3, of which 3 were waited for; matrix products, arithmetic and copies ran while one was open for 3% of the time, Pallas kernels for 0%

profile of v1, /device:TPU:1, one launch (start us, length us, event | category | flops | bytes accessed | tf_op | source)
XLA Modules:
  0.0 620.4 jit_solution(13365061019495883905)
XLA Ops:
  7.3 5.1 stack.2
  12.4 17.0 %all-to-all-start = ((bf16[128,1,64,512]{3,2,1,0:T(8,128)(2,1)}), bf16[128,1,64,512]{3,2,1,0:T(8,128)(2,1)}, u32[]{:S(2)}, u32[]{:S(2)}) async-start(bf16[128,1,64,512]{3,2,1,0:T(8,128)(2,1)} %stack.2), calls=%async_computation | async-start | bytes 16777216 | tf_op jit(solution)/shard_map/all_to_all | solution.py:79
  29.9 201.2 %all-gather.2.cloned.1.call-done = bf16[1,8192,512]{2,1,0:T(8,128)(2,1)} async-done(((bf16[1,64,512]{2,1,0:T(8,128)(2,1)}), bf16[1,8192,512]{2,1,0:T(8,128)(2,1)}) %all-gather.2.cloned.1.call-update) | async-done | bytes 8388624 | tf_op jit(solution)/shard_map/all_gather | solution.py:77
  231.1 11.9 %copy.48 = bf16[1,8192,512]{1,2,0:T(8,128)(2,1)} copy(bf16[1,8192,512]{2,1,0:T(8,128)(2,1)} %all-gather.2.cloned.1.call-done) | data formatting | bytes 16777216 | tf_op jit(solution)/shard_map/while | solution.py:99
  243.0 2.7 all-to-all-done
  250.1 171.5 %collective-permute-done = bf16[64,4096]{1,0:T(8,128)(2,1)S(1)} collective-permute-done((bf16[64,4096]{1,0:T(8,128)(2,1)S(1)}, bf16[64,4096]{1,0:T(8,128)(2,1)S(1)}, u32[]{:S(2)}, u32[]{:S(2)}) %collective-permute-start) | collective-permute-done | bytes 524320 | tf_op jit(solution)/shard_map/ppermute | solution.py:14
  423.1 187.3 %while.39 = (s32[]{:T(128)}, f32[4,8,64]{2,1,0:T(8,128)S(1)}, f32[4,8,64]{2,1,0:T(8,128)S(1)}, f32[64,4,8,128]{3,0,2,1:T(8,128)}, pred[]{:T(512)}, /*index=5*/s3...) while((s32[]{:T(128)}, f32[4,8,64]{2,1,0:T(8,128)S(1)}, ...), condition=%wide.region_14.15_spmd, body=%wide.region_8.14_spmd.sunk | while | flops 549376512 | bytes 37508724 | solution.py:99
  423.2 11.6 %conditional.5 = ((f32[4,8,64]{2,1,0:T(8,128)S(1)}, f32[4,8,64]{2,1,0:T(8,128)S(1)}, f32[64,4,8,128]{3,0,2,1:T(8,128)})) conditional(s32[]{:T(128)} %convert_element_type.110, (f32[4,8,64]{2,1,0:T(8,128)S(1)}, f32[4,8,64]{2,1,0:T(8,128)S(1)}, f32[64,4,8,128]{3,0,2,1:T(8,128)}) %tuple.209, (s32[]{:T(128)}, s32[512,1]{0,1:T(1,128)S(1)}, ...), branch_computations={%region_9.9_spmd, %region_10.13_spmd.clone.clone} | conditional | flops 549376512 | bytes 36980080 | solution.py:54
  428.7 4.8 fusion.32
  434.9 11.6 %conditional.5 = ((f32[4,8,64]{2,1,0:T(8,128)S(1)}, f32[4,8,64]{2,1,0:T(8,128)S(1)}, f32[64,4,8,128]{3,0,2,1:T(8,128)})) conditional(s32[]{:T(128)} %convert_element_type.110, (f32[4,8,64]{2,1,0:T(8,128)S(1)}, f32[4,8,64]{2,1,0:T(8,128)S(1)}, f32[64,4,8,128]{3,0,2,1:T(8,128)}) %tuple.209, (s32[]{:T(128)}, s32[512,1]{0,1:T(1,128)S(1)}, ...), branch_computations={%region_9.9_spmd, %region_10.13_spmd.clone.clone} | conditional | flops 549376512 | bytes 36980080 | solution.py:54
  436.4 2.6 fusion.22
  440.4 4.8 fusion.32
  446.6 11.6 %conditional.5 = ((f32[4,8,64]{2,1,0:T(8,128)S(1)}, f32[4,8,64]{2,1,0:T(8,128)S(1)}, f32[64,4,8,128]{3,0,2,1:T(8,128)})) conditional(s32[]{:T(128)} %convert_element_type.110, (f32[4,8,64]{2,1,0:T(8,128)S(1)}, f32[4,8,64]{2,1,0:T(8,128)S(1)}, f32[64,4,8,128]{3,0,2,1:T(8,128)}) %tuple.209, (s32[]{:T(128)}, s32[512,1]{0,1:T(1,128)S(1)}, ...), branch_computations={%region_9.9_spmd, %region_10.13_spmd.clone.clone} | conditional | flops 549376512 | bytes 36980080 | solution.py:54
  448.1 2.6 fusion.22
  452.1 4.8 fusion.32
  458.3 11.6 %conditional.5 = ((f32[4,8,64]{2,1,0:T(8,128)S(1)}, f32[4,8,64]{2,1,0:T(8,128)S(1)}, f32[64,4,8,128]{3,0,2,1:T(8,128)})) conditional(s32[]{:T(128)} %convert_element_type.110, (f32[4,8,64]{2,1,0:T(8,128)S(1)}, f32[4,8,64]{2,1,0:T(8,128)S(1)}, f32[64,4,8,128]{3,0,2,1:T(8,128)}) %tuple.209, (s32[]{:T(128)}, s32[512,1]{0,1:T(1,128)S(1)}, ...), branch_computations={%region_9.9_spmd, %region_10.13_spmd.clone.clone} | conditional | flops 549376512 | bytes 36980080 | solution.py:54
  463.8 4.8 fusion.32
  470.0 11.6 %conditional.5 = ((f32[4,8,64]{2,1,0:T(8,128)S(1)}, f32[4,8,64]{2,1,0:T(8,128)S(1)}, f32[64,4,8,128]{3,0,2,1:T(8,128)})) conditional(s32[]{:T(128)} %convert_element_type.110, (f32[4,8,64]{2,1,0:T(8,128)S(1)}, f32[4,8,64]{2,1,0:T(8,128)S(1)}, f32[64,4,8,128]{3,0,2,1:T(8,128)}) %tuple.209, (s32[]{:T(128)}, s32[512,1]{0,1:T(1,128)S(1)}, ...), branch_computations={%region_9.9_spmd, %region_10.13_spmd.clone.clone} | conditional | flops 549376512 | bytes 36980080 | solution.py:54
  471.5 2.6 fusion.22
  475.5 4.8 fusion.32
  481.7 11.6 %conditional.5 = ((f32[4,8,64]{2,1,0:T(8,128)S(1)}, f32[4,8,64]{2,1,0:T(8,128)S(1)}, f32[64,4,8,128]{3,0,2,1:T(8,128)})) conditional(s32[]{:T(128)} %convert_element_type.110, (f32[4,8,64]{2,1,0:T(8,128)S(1)}, f32[4,8,64]{2,1,0:T(8,128)S(1)}, f32[64,4,8,128]{3,0,2,1:T(8,128)}) %tuple.209, (s32[]{:T(128)}, s32[512,1]{0,1:T(1,128)S(1)}, ...), branch_computations={%region_9.9_spmd, %region_10.13_spmd.clone.clone} | conditional | flops 549376512 | bytes 36980080 | solution.py:54
  483.2 2.6 fusion.22
  487.2 4.8 fusion.32
  493.4 11.6 %conditional.5 = ((f32[4,8,64]{2,1,0:T(8,128)S(1)}, f32[4,8,64]{2,1,0:T(8,128)S(1)}, f32[64,4,8,128]{3,0,2,1:T(8,128)})) conditional(s32[]{:T(128)} %convert_element_type.110, (f32[4,8,64]{2,1,0:T(8,128)S(1)}, f32[4,8,64]{2,1,0:T(8,128)S(1)}, f32[64,4,8,128]{3,0,2,1:T(8,128)}) %tuple.209, (s32[]{:T(128)}, s32[512,1]{0,1:T(1,128)S(1)}, ...), branch_computations={%region_9.9_spmd, %region_10.13_spmd.clone.clone} | conditional | flops 549376512 | bytes 36980080 | solution.py:54
  494.9 2.6 fusion.22
  498.9 4.8 fusion.32
  505.2 11.6 %conditional.5 = ((f32[4,8,64]{2,1,0:T(8,128)S(1)}, f32[4,8,64]{2,1,0:T(8,128)S(1)}, f32[64,4,8,128]{3,0,2,1:T(8,128)})) conditional(s32[]{:T(128)} %convert_element_type.110, (f32[4,8,64]{2,1,0:T(8,128)S(1)}, f32[4,8,64]{2,1,0:T(8,128)S(1)}, f32[64,4,8,128]{3,0,2,1:T(8,128)}) %tuple.209, (s32[]{:T(128)}, s32[512,1]{0,1:T(1,128)S(1)}, ...), branch_computations={%region_9.9_spmd, %region_10.13_spmd.clone.clone} | conditional | flops 549376512 | bytes 36980080 | solution.py:54
  510.6 4.8 fusion.32
  516.9 11.6 %conditional.5 = ((f32[4,8,64]{2,1,0:T(8,128)S(1)}, f32[4,8,64]{2,1,0:T(8,128)S(1)}, f32[64,4,8,128]{3,0,2,1:T(8,128)})) conditional(s32[]{:T(128)} %convert_element_type.110, (f32[4,8,64]{2,1,0:T(8,128)S(1)}, f32[4,8,64]{2,1,0:T(8,128)S(1)}, f32[64,4,8,128]{3,0,2,1:T(8,128)}) %tuple.209, (s32[]{:T(128)}, s32[512,1]{0,1:T(1,128)S(1)}, ...), branch_computations={%region_9.9_spmd, %region_10.13_spmd.clone.clone} | conditional | flops 549376512 | bytes 36980080 | solution.py:54
  518.3 2.6 fusion.22
  522.3 4.8 fusion.32
  528.6 11.6 %conditional.5 = ((f32[4,8,64]{2,1,0:T(8,128)S(1)}, f32[4,8,64]{2,1,0:T(8,128)S(1)}, f32[64,4,8,128]{3,0,2,1:T(8,128)})) conditional(s32[]{:T(128)} %convert_element_type.110, (f32[4,8,64]{2,1,0:T(8,128)S(1)}, f32[4,8,64]{2,1,0:T(8,128)S(1)}, f32[64,4,8,128]{3,0,2,1:T(8,128)}) %tuple.209, (s32[]{:T(128)}, s32[512,1]{0,1:T(1,128)S(1)}, ...), branch_computations={%region_9.9_spmd, %region_10.13_spmd.clone.clone} | conditional | flops 549376512 | bytes 36980080 | solution.py:54
  534.0 4.8 fusion.32
  540.3 11.6 %conditional.5 = ((f32[4,8,64]{2,1,0:T(8,128)S(1)}, f32[4,8,64]{2,1,0:T(8,128)S(1)}, f32[64,4,8,128]{3,0,2,1:T(8,128)})) conditional(s32[]{:T(128)} %convert_element_type.110, (f32[4,8,64]{2,1,0:T(8,128)S(1)}, f32[4,8,64]{2,1,0:T(8,128)S(1)}, f32[64,4,8,128]{3,0,2,1:T(8,128)}) %tuple.209, (s32[]{:T(128)}, s32[512,1]{0,1:T(1,128)S(1)}, ...), branch_computations={%region_9.9_spmd, %region_10.13_spmd.clone.clone} | conditional | flops 549376512 | bytes 36980080 | solution.py:54
  541.7 2.6 fusion.22
  545.7 4.8 fusion.32
  552.0 11.6 %conditional.5 = ((f32[4,8,64]{2,1,0:T(8,128)S(1)}, f32[4,8,64]{2,1,0:T(8,128)S(1)}, f32[64,4,8,128]{3,0,2,1:T(8,128)})) conditional(s32[]{:T(128)} %convert_element_type.110, (f32[4,8,64]{2,1,0:T(8,128)S(1)}, f32[4,8,64]{2,1,0:T(8,128)S(1)}, f32[64,4,8,128]{3,0,2,1:T(8,128)}) %tuple.209, (s32[]{:T(128)}, s32[512,1]{0,1:T(1,128)S(1)}, ...), branch_computations={%region_9.9_spmd, %region_10.13_spmd.clone.clone} | conditional | flops 549376512 | bytes 36980080 | solution.py:54
  557.4 4.8 fusion.32
  563.7 11.6 %conditional.5 = ((f32[4,8,64]{2,1,0:T(8,128)S(1)}, f32[4,8,64]{2,1,0:T(8,128)S(1)}, f32[64,4,8,128]{3,0,2,1:T(8,128)})) conditional(s32[]{:T(128)} %convert_element_type.110, (f32[4,8,64]{2,1,0:T(8,128)S(1)}, f32[4,8,64]{2,1,0:T(8,128)S(1)}, f32[64,4,8,128]{3,0,2,1:T(8,128)}) %tuple.209, (s32[]{:T(128)}, s32[512,1]{0,1:T(1,128)S(1)}, ...), branch_computations={%region_9.9_spmd, %region_10.13_spmd.clone.clone} | conditional | flops 549376512 | bytes 36980080 | solution.py:54
  565.2 2.6 fusion.22
  569.1 4.8 fusion.32
  575.4 11.6 %conditional.5 = ((f32[4,8,64]{2,1,0:T(8,128)S(1)}, f32[4,8,64]{2,1,0:T(8,128)S(1)}, f32[64,4,8,128]{3,0,2,1:T(8,128)})) conditional(s32[]{:T(128)} %convert_element_type.110, (f32[4,8,64]{2,1,0:T(8,128)S(1)}, f32[4,8,64]{2,1,0:T(8,128)S(1)}, f32[64,4,8,128]{3,0,2,1:T(8,128)}) %tuple.209, (s32[]{:T(128)}, s32[512,1]{0,1:T(1,128)S(1)}, ...), branch_computations={%region_9.9_spmd, %region_10.13_spmd.clone.clone} | conditional | flops 549376512 | bytes 36980080 | solution.py:54
  580.8 4.8 fusion.32
  587.1 11.6 %conditional.5 = ((f32[4,8,64]{2,1,0:T(8,128)S(1)}, f32[4,8,64]{2,1,0:T(8,128)S(1)}, f32[64,4,8,128]{3,0,2,1:T(8,128)})) conditional(s32[]{:T(128)} %convert_element_type.110, (f32[4,8,64]{2,1,0:T(8,128)S(1)}, f32[4,8,64]{2,1,0:T(8,128)S(1)}, f32[64,4,8,128]{3,0,2,1:T(8,128)}) %tuple.209, (s32[]{:T(128)}, s32[512,1]{0,1:T(1,128)S(1)}, ...), branch_computations={%region_9.9_spmd, %region_10.13_spmd.clone.clone} | conditional | flops 549376512 | bytes 36980080 | solution.py:54
  588.6 2.6 fusion.22
  592.5 4.8 fusion.32
  598.8 11.6 %conditional.5 = ((f32[4,8,64]{2,1,0:T(8,128)S(1)}, f32[4,8,64]{2,1,0:T(8,128)S(1)}, f32[64,4,8,128]{3,0,2,1:T(8,128)})) conditional(s32[]{:T(128)} %convert_element_type.110, (f32[4,8,64]{2,1,0:T(8,128)S(1)}, f32[4,8,64]{2,1,0:T(8,128)S(1)}, f32[64,4,8,128]{3,0,2,1:T(8,128)}) %tuple.209, (s32[]{:T(128)}, s32[512,1]{0,1:T(1,128)S(1)}, ...), branch_computations={%region_9.9_spmd, %region_10.13_spmd.clone.clone} | conditional | flops 549376512 | bytes 36980080 | solution.py:54
  604.2 4.8 fusion.32
  (359 shorter events, 95.2 us)
Async XLA Ops:
  6.5 224.6 %all-gather.2.cloned.1.call-start = ((), (), s32[]{:S(2)}) async-start(), calls=%async_computation.1 | async-start | bytes 8454144 | tf_op jit(solution)/shard_map/all_gather | solution.py:77
  12.4 17.0 %copy-start.2 = (bf16[1,64,4096]{2,1,0:T(8,128)(2,1)S(1)}, bf16[1,64,4096]{2,1,0:T(8,128)(2,1)}, u32[]{:S(2)}) copy-start(bf16[1,64,4096]{2,1,0:T(8,128)(2,1)} %param.13) | copy-start | bytes 1572868
  12.4 17.4 %copy-start.3 = (s32[256]{0:T(256)S(1)}, s32[256]{0:T(256)}, u32[]{:S(2)}) copy-start(s32[256]{0:T(256)} %param.17) | copy-start | bytes 3076
  12.4 233.4 %all-to-all-start = ((bf16[128,1,64,512]{3,2,1,0:T(8,128)(2,1)}), bf16[128,1,64,512]{3,2,1,0:T(8,128)(2,1)}, u32[]{:S(2)}, u32[]{:S(2)}) async-start(bf16[128,1,64,512]{3,2,1,0:T(8,128)(2,1)} %stack.2), calls=%async_computation | async-start | bytes 16777216 | tf_op jit(solution)/shard_map/all_to_all | solution.py:79
  245.9 175.7 %copy-start.4 = (f32[4096]{0:T(1024)S(1)}, f32[4096]{0:T(1024)}, u32[]{:S(2)}) copy-start(f32[4096]{0:T(1024)} %param.16) | copy-start | bytes 49156
  248.6 173.0 %collective-permute-start = (bf16[64,4096]{1,0:T(8,128)(2,1)S(1)}, bf16[64,4096]{1,0:T(8,128)(2,1)S(1)}, u32[]{:S(2)}, u32[]{:S(2)}) collective-permute-start(bf16[64,4096]{1,0:T(8,128)(2,1)S(1)} %bitcast.115), channel_id=1, source_target_pairs={{0,128},{1,129},{2,130},{3,131},{4,132},{5,133},{6,134},{7,135},{8... | collective-permute-start | bytes 1572872 | tf_op jit(solution)/shard_map/ppermute | solution.py:14
  428.6 4.8 copy-start.1
  440.3 4.8 copy-start.1
  452.1 4.8 copy-start.1
  463.8 4.8 copy-start.1
  475.5 4.8 copy-start.1
  487.2 4.8 copy-start.1
  498.9 4.8 copy-start.1
  510.6 4.8 copy-start.1
  522.3 4.8 copy-start.1
  534.0 4.8 copy-start.1
  545.7 4.8 copy-start.1
  557.4 4.8 copy-start.1
  569.1 4.8 copy-start.1
  580.8 4.8 copy-start.1
  592.5 4.8 copy-start.1
  604.2 4.8 copy-start.1
Sparse Core Ops, SparseCore 0:
  11.0 220.0 all-gather.1
